TPU v7x, 32 devices: a whole 2x2x4 slice. The times are simulated.
32 devices in a mesh: dp: 16 (over z, y, core), tensor: 2 (over x).
Axes of the slice: x: 2, y: 2, z: 4, core: 2. Of those that a mesh axis runs over, the one named last changes fastest.
Arguments:
- tokens: bfloat16 [16384, 768], P(('dp', 'tensor')), may hold values from -6 to 6
- query_weight: bfloat16 [768, 768], P('dp', 'tensor'), may hold values from -0.21875 to 0.21875
- query_bias: float32 [768], replicated, may hold values from -3 to 3
- key_weight: bfloat16 [768, 768], P('dp', 'tensor'), may hold values from -0.21875 to 0.21875
- value_weight: bfloat16 [768, 768], P('dp', 'tensor'), may hold values from -0.21875 to 0.21875
- value_bias: float32 [768], replicated, may hold values from -0.625 to 0.625
- output_weight: bfloat16 [768, 768], P('tensor', 'dp'), may hold values from -1.25 to 1.25
- output_bias: float32 [768], replicated, may hold values from -3 to 3
- first_gain: float32 [768], replicated, may hold values from 0.5 to 1.5
- first_shift: float32 [768], replicated, may hold values from -3 to 3
- inner_weight: bfloat16 [768, 3072], P('dp', 'tensor'), may hold values from -0.21875 to 0.21875
- inner_bias: float32 [3072], replicated, may hold values from -3 to 3
- outer_weight: bfloat16 [3072, 768], P('tensor', 'dp'), may hold values from -0.109375 to 0.109375
- outer_bias: float32 [768], replicated, may hold values from -3 to 3
- second_gain: float32 [768], replicated, may hold values from 0.5 to 1.5
- second_shift: float32 [768], replicated, may hold values from -3 to 3
- segments: int32 [16, 1024], P('dp'), may hold values from 0 to 7, never falling along the last dimension, each value on 1 to 768 neighbouring positions
- valid_length: int32 [16], P('dp'), may hold values from 512 to 1024
- cotangent: bfloat16 [16384, 768], P(('dp', 'tensor')), may hold values from -6 to 6
Outputs:
- layer_output: bfloat16 [16384, 768], P(('dp', 'tensor'))
- input_gradient: float32 [16384, 768], P(('dp', 'tensor'))
- query_weight_gradient: float32 [768, 768], P('dp', 'tensor')
- query_bias_gradient: float32 [768], replicated
- key_weight_gradient: float32 [768, 768], P('dp', 'tensor')
- value_weight_gradient: float32 [768, 768], P('dp', 'tensor')
- value_bias_gradient: float32 [768], replicated
- output_weight_gradient: float32 [768, 768], P('tensor', 'dp')
- output_bias_gradient: float32 [768], replicated
- first_gain_gradient: float32 [768], replicated
- first_shift_gradient: float32 [768], replicated
- inner_weight_gradient: float32 [768, 3072], P('dp', 'tensor')
- inner_bias_gradient: float32 [3072], replicated
- outer_weight_gradient: float32 [3072, 768], P('tensor', 'dp')
- outer_bias_gradient: float32 [768], replicated
- second_gain_gradient: float32 [768], replicated
- second_shift_gradient: float32 [768], replicated
Inputs may be any that keep to these rules, and one draw needn't show every extreme that they name: `segments`: segment numbers never fall along a sequence; a token attends only to tokens of its own document. tokens of a sequence at positions valid_length and beyond are padding: no query attends to them as keys except the token itself.
All inputs are finite; a program needn't handle non-finite values.
Results may differ from a plain program's by a relative error of at most 0.013.
Values may be sent and summed in bfloat16 or wider, within the bound.
No kernel may reach another device: no remote copies, remote signals or barrier semaphores. Data moves between devices by JAX's collectives and lax.ppermute only.
A program may use at most 128 MiB of HBM per device.

v0:
```python
import jax
import jax.numpy as jnp
from jax import lax
from jax.sharding import PartitionSpec as P

HEAD_DIM = 64
norm_epsilon = 1e-12
masked_score = -1e30


def normalize(matrix, gain, shift):
    center = matrix - jnp.mean(matrix, axis=-1, keepdims=True)
    spread = jnp.mean(center * center, axis=-1, keepdims=True)
    return center * lax.rsqrt(spread + norm_epsilon) * gain + shift


def exact_gelu(inner):
    return jax.nn.gelu(inner, approximate=False)


def block_scores(query_block, key_seq, segment_row, valid_count, first_row):
    block_rows = query_block.shape[0]
    length = key_seq.shape[0]
    scores = (
        jnp.einsum("qhd,khd->hqk", query_block, key_seq, preferred_element_type=jnp.float32) * 0.125
    )
    positions = jnp.arange(length, dtype=jnp.int32)
    query_pos = first_row + jnp.arange(block_rows, dtype=jnp.int32)
    query_seg = lax.dynamic_slice_in_dim(segment_row, first_row, block_rows)
    allowed = (query_seg[:, None] == segment_row[None, :]) & (
        (positions[None, :] < valid_count) | (query_pos[:, None] == positions[None, :])
    )
    return jnp.where(allowed[None], scores, masked_score)


def attend_sequence(pieces):
    query_seq, key_seq, value_seq, segment_row, valid_count = pieces
    length = query_seq.shape[0]
    block_rows = min(512, length)

    def one_block(block_index):
        first_row = block_index * block_rows
        query_block = lax.dynamic_slice_in_dim(query_seq, first_row, block_rows)
        masked = block_scores(query_block, key_seq, segment_row, valid_count, first_row)
        largest = jnp.max(masked, axis=-1, keepdims=True)
        totals = jnp.sum(jnp.exp(masked - largest), axis=-1, keepdims=True)
        log_total = largest + jnp.log(totals)
        probs_low = jnp.exp(masked - log_total).astype(jnp.bfloat16)
        context = jnp.einsum(
            "hqk,khd->qhd", probs_low, value_seq, preferred_element_type=jnp.float32
        )
        return (context.astype(jnp.bfloat16), log_total[..., 0])

    contexts, log_totals = lax.map(one_block, jnp.arange(length // block_rows, dtype=jnp.int32))
    return (contexts.reshape(query_seq.shape), log_totals)


def attend_backward(pieces):
    query_seq, key_seq, value_seq, segment_row, valid_count, grad_seq, log_totals = pieces
    length = query_seq.shape[0]
    block_rows = min(512, length)

    def one_block(running, inputs):
        key_grad, value_grad = running
        block_index, log_total = inputs
        first_row = block_index * block_rows
        query_block = lax.dynamic_slice_in_dim(query_seq, first_row, block_rows)
        grad_block = lax.dynamic_slice_in_dim(grad_seq, first_row, block_rows)
        masked = block_scores(query_block, key_seq, segment_row, valid_count, first_row)
        probs = jnp.exp(masked - log_total[..., None])
        probs_low = probs.astype(jnp.bfloat16)
        value_grad = value_grad + jnp.einsum(
            "hqk,qhd->khd", probs_low, grad_block, preferred_element_type=jnp.float32
        )
        d_probs = jnp.einsum(
            "qhd,khd->hqk", grad_block, value_seq, preferred_element_type=jnp.float32
        )
        row_inner = jnp.sum(probs * d_probs, axis=-1, keepdims=True)
        d_scores = (probs * (d_probs - row_inner)).astype(jnp.bfloat16)
        query_grad = (
            jnp.einsum("hqk,khd->qhd", d_scores, key_seq, preferred_element_type=jnp.float32)
            * 0.125
        )
        key_grad = (
            key_grad
            + jnp.einsum("hqk,qhd->khd", d_scores, query_block, preferred_element_type=jnp.float32)
            * 0.125
        )
        return ((key_grad, value_grad), query_grad.astype(jnp.bfloat16))

    empty = jnp.zeros(key_seq.shape, jnp.float32)
    block_ids = jnp.arange(length // block_rows, dtype=jnp.int32)
    (key_grad, value_grad), query_grads = lax.scan(
        one_block, (empty, empty), (block_ids, log_totals)
    )
    return (
        query_grads.reshape(query_seq.shape),
        key_grad.astype(jnp.bfloat16),
        value_grad.astype(jnp.bfloat16),
    )


def place_vector(local_part, whole, shard_index):
    width = local_part.shape[0]
    return lax.dynamic_update_slice_in_dim(
        jnp.zeros((whole,), jnp.float32), local_part, shard_index * width, 0
    )


def on_device(
    tokens,
    query_weight,
    query_bias,
    key_weight,
    value_weight,
    value_bias,
    output_weight,
    output_bias,
    first_gain,
    first_shift,
    inner_weight,
    inner_bias,
    outer_weight,
    outer_bias,
    second_gain,
    second_shift,
    segments,
    valid_length,
    cotangent,
):
    head_cols = query_weight.shape[1]
    hidden_cols = inner_weight.shape[1]
    local_heads = head_cols // HEAD_DIM
    shard_index = lax.axis_index("tensor")
    bias_query = lax.dynamic_slice_in_dim(query_bias, shard_index * head_cols, head_cols)
    bias_value = lax.dynamic_slice_in_dim(value_bias, shard_index * head_cols, head_cols)
    bias_inner = lax.dynamic_slice_in_dim(inner_bias, shard_index * hidden_cols, hidden_cols)
    full_query, full_key, full_value, full_output, full_inner, full_outer = (
        lax.all_gather(query_weight, "dp", axis=0, tiled=True),
        lax.all_gather(key_weight, "dp", axis=0, tiled=True),
        lax.all_gather(value_weight, "dp", axis=0, tiled=True),
        lax.all_gather(output_weight, "dp", axis=1, tiled=True),
        lax.all_gather(inner_weight, "dp", axis=0, tiled=True),
        lax.all_gather(outer_weight, "dp", axis=1, tiled=True),
    )
    group_rows = lax.all_gather(tokens, "tensor", axis=0, tiled=True)
    seq_count = segments.shape[0]
    seq_length = segments.shape[1]
    four_shape = (seq_count, seq_length, local_heads, HEAD_DIM)
    queries = (
        jnp.dot(group_rows, full_query, preferred_element_type=jnp.float32) + bias_query
    ).astype(jnp.bfloat16)
    keys_all = jnp.dot(group_rows, full_key, preferred_element_type=jnp.float32).astype(
        jnp.bfloat16
    )
    values_all = (
        jnp.dot(group_rows, full_value, preferred_element_type=jnp.float32) + bias_value
    ).astype(jnp.bfloat16)
    queries = queries.reshape(four_shape)
    keys_all = keys_all.reshape(four_shape)
    values_all = values_all.reshape(four_shape)
    contexts, log_totals = lax.map(
        attend_sequence, (queries, keys_all, values_all, segments, valid_length)
    )
    context = contexts.reshape(seq_count * seq_length, head_cols)
    partial_attn = jnp.dot(context, full_output, preferred_element_type=jnp.float32)
    attended = lax.psum_scatter(partial_attn, "tensor", scatter_dimension=0, tiled=True)
    first_sum = tokens.astype(jnp.float32) + attended + output_bias
    hidden = normalize(first_sum, first_gain, first_shift)
    ffn_rows = lax.all_gather(hidden.astype(jnp.bfloat16), "tensor", axis=0, tiled=True)
    inner = jnp.dot(ffn_rows, full_inner, preferred_element_type=jnp.float32) + bias_inner
    activated = exact_gelu(inner).astype(jnp.bfloat16)
    partial_ffn = jnp.dot(activated, full_outer, preferred_element_type=jnp.float32)
    outer = lax.psum_scatter(partial_ffn, "tensor", scatter_dimension=0, tiled=True)
    second_sum = hidden + outer + outer_bias
    final = normalize(second_sum, second_gain, second_shift)
    layer_output = final.astype(jnp.bfloat16)
    second_value, second_pull = jax.vjp(normalize, second_sum, second_gain, second_shift)
    d_second, second_gain_grad, second_shift_grad = second_pull(cotangent.astype(jnp.float32))
    outer_bias_grad = jnp.sum(d_second, axis=0)
    d_outer = d_second.astype(jnp.bfloat16)
    held = lax.optimization_barrier(
        (query_weight, key_weight, value_weight, output_weight, inner_weight, outer_weight, d_outer)
    )
    d_outer = held[6]
    back_query, back_key, back_value, back_output, back_inner, back_outer = (
        lax.all_gather(held[0], "dp", axis=0, tiled=True),
        lax.all_gather(held[1], "dp", axis=0, tiled=True),
        lax.all_gather(held[2], "dp", axis=0, tiled=True),
        lax.all_gather(held[3], "dp", axis=1, tiled=True),
        lax.all_gather(held[4], "dp", axis=0, tiled=True),
        lax.all_gather(held[5], "dp", axis=1, tiled=True),
    )
    outer_grad_rows = lax.all_gather(d_outer, "tensor", axis=0, tiled=True)
    outer_weight_grad = jnp.einsum(
        "gf,gd->fd", activated, outer_grad_rows, preferred_element_type=jnp.float32
    )
    d_activated = jnp.einsum(
        "gd,fd->gf", outer_grad_rows, back_outer, preferred_element_type=jnp.float32
    )
    gelu_value, gelu_pull = jax.vjp(exact_gelu, inner)
    d_inner = gelu_pull(d_activated)[0].astype(jnp.bfloat16)
    inner_weight_grad = jnp.einsum(
        "gd,gf->df", ffn_rows, d_inner, preferred_element_type=jnp.float32
    )
    inner_bias_local = jnp.sum(d_inner, axis=0, dtype=jnp.float32)
    partial_hidden = jnp.einsum(
        "gf,df->gd", d_inner, back_inner, preferred_element_type=jnp.float32
    )
    d_hidden = d_second + lax.psum_scatter(
        partial_hidden, "tensor", scatter_dimension=0, tiled=True
    )
    first_value, first_pull = jax.vjp(normalize, first_sum, first_gain, first_shift)
    d_first, first_gain_grad, first_shift_grad = first_pull(d_hidden)
    output_bias_grad = jnp.sum(d_first, axis=0)
    attn_grad_rows = lax.all_gather(d_first.astype(jnp.bfloat16), "tensor", axis=0, tiled=True)
    output_weight_grad = jnp.einsum(
        "gc,gd->cd", context, attn_grad_rows, preferred_element_type=jnp.float32
    )
    d_context = jnp.einsum(
        "gd,cd->gc", attn_grad_rows, back_output, preferred_element_type=jnp.float32
    ).astype(jnp.bfloat16)
    d_queries, d_keys, d_values = lax.map(
        attend_backward,
        (
            queries,
            keys_all,
            values_all,
            segments,
            valid_length,
            d_context.reshape(four_shape),
            log_totals,
        ),
    )
    d_queries = d_queries.reshape(seq_count * seq_length, head_cols)
    d_keys = d_keys.reshape(seq_count * seq_length, head_cols)
    d_values = d_values.reshape(seq_count * seq_length, head_cols)
    query_weight_grad = jnp.einsum(
        "gd,gc->dc", group_rows, d_queries, preferred_element_type=jnp.float32
    )
    key_weight_grad = jnp.einsum(
        "gd,gc->dc", group_rows, d_keys, preferred_element_type=jnp.float32
    )
    value_weight_grad = jnp.einsum(
        "gd,gc->dc", group_rows, d_values, preferred_element_type=jnp.float32
    )
    query_bias_local = jnp.sum(d_queries, axis=0, dtype=jnp.float32)
    value_bias_local = jnp.sum(d_values, axis=0, dtype=jnp.float32)
    partial_input = jnp.einsum(
        "gc,dc->gd", d_queries, back_query, preferred_element_type=jnp.float32
    )
    partial_input = partial_input + jnp.einsum(
        "gc,dc->gd", d_keys, back_key, preferred_element_type=jnp.float32
    )
    partial_input = partial_input + jnp.einsum(
        "gc,dc->gd", d_values, back_value, preferred_element_type=jnp.float32
    )
    input_gradient = d_first + lax.psum_scatter(
        partial_input.astype(jnp.bfloat16), "tensor", scatter_dimension=0, tiled=True
    ).astype(jnp.float32)
    query_shard, key_shard, value_shard, output_shard, inner_shard, outer_shard = (
        lax.psum_scatter(query_weight_grad, "dp", scatter_dimension=0, tiled=True),
        lax.psum_scatter(key_weight_grad, "dp", scatter_dimension=0, tiled=True),
        lax.psum_scatter(value_weight_grad, "dp", scatter_dimension=0, tiled=True),
        lax.psum_scatter(output_weight_grad, "dp", scatter_dimension=1, tiled=True),
        lax.psum_scatter(inner_weight_grad, "dp", scatter_dimension=0, tiled=True),
        lax.psum_scatter(outer_weight_grad, "dp", scatter_dimension=1, tiled=True),
    )
    model_width = query_bias.shape[0]
    hidden_width = inner_bias.shape[0]
    query_bias_full = place_vector(query_bias_local, model_width, shard_index)
    value_bias_full = place_vector(value_bias_local, model_width, shard_index)
    inner_bias_full = place_vector(inner_bias_local, hidden_width, shard_index)
    summed = lax.psum(
        (
            query_bias_full,
            value_bias_full,
            output_bias_grad,
            first_gain_grad,
            first_shift_grad,
            inner_bias_full,
            outer_bias_grad,
            second_gain_grad,
            second_shift_grad,
        ),
        ("dp", "tensor"),
    )
    return (
        layer_output,
        input_gradient,
        query_shard,
        summed[0],
        key_shard,
        value_shard,
        summed[1],
        output_shard,
        summed[2],
        summed[3],
        summed[4],
        inner_shard,
        summed[5],
        outer_shard,
        summed[6],
        summed[7],
        summed[8],
    )


def solution(mesh):
    placed = (
        P(("dp", "tensor"), None),
        P("dp", "tensor"),
        P(),
        P("dp", "tensor"),
        P("dp", "tensor"),
        P(),
        P("tensor", "dp"),
        P(),
        P(),
        P(),
        P("dp", "tensor"),
        P(),
        P("tensor", "dp"),
        P(),
        P(),
        P(),
        P("dp", None),
        P("dp"),
        P(("dp", "tensor"), None),
    )
    return jax.shard_map(
        on_device,
        mesh=mesh,
        in_specs=placed,
        out_specs=(
            P(("dp", "tensor"), None),
            P(("dp", "tensor"), None),
            P("dp", "tensor"),
            P(),
            P("dp", "tensor"),
            P("dp", "tensor"),
            P(),
            P("tensor", "dp"),
            P(),
            P(),
            P(),
            P("dp", "tensor"),
            P(),
            P("tensor", "dp"),
            P(),
            P(),
            P(),
        ),
        check_vma=False,
    )
```

profile of v0, /device:TPU:0, one launch (start us, length us, event | category | flops | bytes accessed | tf_op | source)
XLA Modules:
  0.0 1077.9 jit_solution(17472114728465103642)
XLA Ops:
  10.3 25.1 %all_gather.49 = bf16[768,384]{1,0:T(8,128)(2,1)S(1)} all-gather(bf16[48,384]{1,0:T(8,128)(2,1)} %param.24), channel_id=1, replica_groups=mesh['dp'=16,'tensor'=2] {'dp'}, dimensions={0}, use_global_device_ids=true | all-gather | bytes 626688 | tf_op jit(solution)/shard_map/all_gather | solution.py:139
  35.4 19.3 %all_gather.50 = bf16[768,384]{1,0:T(8,128)(2,1)S(1)} all-gather(bf16[48,384]{1,0:T(8,128)(2,1)} %param.26), channel_id=1, replica_groups=mesh['dp'=16,'tensor'=2] {'dp'}, dimensions={0}, use_global_device_ids=true | all-gather | bytes 626688 | tf_op jit(solution)/shard_map/all_gather | solution.py:140
  54.7 20.7 %all_gather.51 = bf16[768,384]{1,0:T(8,128)(2,1)S(1)} all-gather(bf16[48,384]{1,0:T(8,128)(2,1)} %param.27), channel_id=1, replica_groups=mesh['dp'=16,'tensor'=2] {'dp'}, dimensions={0}, use_global_device_ids=true | all-gather | bytes 626688 | tf_op jit(solution)/shard_map/all_gather | solution.py:141
  75.4 20.7 %all_gather.52 = bf16[384,768]{0,1:T(8,128)(2,1)} all-gather(bf16[384,48]{0,1:T(8,128)(2,1)} %param.29), channel_id=1, replica_groups=mesh['dp'=16,'tensor'=2] {'dp'}, dimensions={1}, use_global_device_ids=true | all-gather | bytes 626688 | tf_op jit(solution)/shard_map/all_gather | solution.py:142
  100.2 34.8 %while.47 = (s32[]{:T(128)}, bf16[2,512,6,64]{1,3,2,0:T(8,128)(2,1)S(1)}, f32[2,6,512]{2,1,0:T(8,128)S(1)}, s32[2]{0:T(128)S(1)}, s32[1024]{0:T(1024)S(1)}, /*in...) while((s32[]{:T(128)}, ...), condition=%wide.region_3.4_spmd, body=%wide.region_0.3_spmd.sunk | while | flops 842201600 | bytes 92672240 | solution.py:54
  105.3 3.6 exponential_reduce_fusion.2
  109.8 7.8 fusion.126
  122.7 3.6 exponential_reduce_fusion.2
  127.3 7.8 fusion.126
  140.5 41.1 %reduce-scatter.17.cloned.1.call-done = f32[512,768]{1,0:T(8,128)} async-done(((f32[1024,768]{1,0:T(8,128)}), f32[512,768]{1,0:T(8,128)}) %reduce-scatter.17.cloned.1.call-update) | async-done | bytes 1572880 | tf_op jit(solution)/shard_map/reduce_scatter | solution.py:167
  185.7 26.4 %all-gather.11.cloned.1.call-done = bf16[1024,768]{1,0:T(8,128)(2,1)} async-done(((bf16[512,768]{1,0:T(8,128)(2,1)}), bf16[1024,768]{1,0:T(8,128)(2,1)}) %all-gather.11.cloned.1.call-update) | async-done | bytes 1572880 | tf_op jit(solution)/shard_map/all_gather | solution.py:170
  212.1 19.9 %multiply_convert_fusion.1 = (bf16[1024,1536]{1,0:T(8,128)(2,1)}, f32[1024,1536]{1,0:T(8,128)}, f32[1024,1536]{1,0:T(8,128)}) fusion(f32[1536]{0:T(1024)S(1)} %dynamic_slice.65, bf16[1024,768]{1,0:T(8,128)(2,1)} %all-gather.11.cloned.1.call-done, bf16[768,1536]{1,0:T(8,128)(2,1)} %all-gather.13.cloned.1.call-done), kind=kOutput, calls=%fused_computation.55 | convolution fusion | flops 2519728128 | bytes 19666944 | tf_op jit(solution)/shard_map/dot_general | solution.py:171
  232.0 24.9 %all-gather.15.cloned.1.call-done = bf16[1536,768]{0,1:T(8,128)(2,1)} async-done(((bf16[1536,48]{0,1:T(8,128)(2,1)}), bf16[1536,768]{0,1:T(8,128)(2,1)}) %all-gather.15.cloned.1.call-update) | async-done | bytes 2359312 | tf_op jit(solution)/shard_map/all_gather | solution.py:144
  256.9 6.9 fusion.55
  263.9 41.9 %reduce-scatter.19.cloned.1.call-done = f32[512,768]{1,0:T(8,128)} async-done(((f32[1024,768]{1,0:T(8,128)}), f32[512,768]{1,0:T(8,128)}) %reduce-scatter.19.cloned.1.call-update) | async-done | bytes 1572880 | tf_op jit(solution)/shard_map/reduce_scatter | solution.py:174
  315.8 25.2 %all-gather.17.cloned.1.call-done = bf16[1024,768]{1,0:T(8,128)(2,1)} async-done(((bf16[512,768]{1,0:T(8,128)(2,1)}), bf16[1024,768]{1,0:T(8,128)(2,1)}) %all-gather.17.cloned.1.call-update) | async-done | bytes 1572880 | tf_op jit(solution)/shard_map/all_gather | solution.py:194
  341.0 45.0 %all-gather.19.cloned.1.call-done = bf16[1536,768]{0,1:T(8,128)(2,1)} async-done(((bf16[1536,48]{0,1:T(8,128)(2,1)}), bf16[1536,768]{0,1:T(8,128)(2,1)}) %all-gather.19.cloned.1.call-update) | async-done | bytes 2359312 | tf_op jit(solution)/shard_map/all_gather | solution.py:192
  385.9 12.4 %convert_reduce_fusion = (f32[1536]{0:T(1024)}, bf16[1024,1536]{1,0:T(8,128)(2,1)}) fusion(f32[1024,1536]{1,0:T(8,128)} %get-tuple-element.366, f32[1024,1536]{1,0:T(8,128)} %get-tuple-element.378, f32[1536]{0:T(1024)S(1)} %dynamic_slice.65, bf16[1024,768]{1,0:T(8,128)(2,1)} %all-gather.17.cloned.1.call-done, ...), kind=kOutput, calls=%fused_computation.53 | convolution fusion | flops 2442656256 | bytes 19673088 | tf_op jit(solution)/shard_map/gd,fd->gf/dot_general | solution.py:198
  398.4 30.9 %all-gather.21.cloned.1.call-done = bf16[768,1536]{1,0:T(8,128)(2,1)} async-done(((bf16[48,1536]{1,0:T(8,128)(2,1)}), bf16[768,1536]{1,0:T(8,128)(2,1)}) %all-gather.21.cloned.1.call-update) | async-done | bytes 2359312 | tf_op jit(solution)/shard_map/all_gather | solution.py:191
  429.3 6.9 fusion.56
  436.2 41.9 %reduce-scatter.21.cloned.1.call-done = f32[512,768]{1,0:T(8,128)} async-done(((f32[1024,768]{1,0:T(8,128)}), f32[512,768]{1,0:T(8,128)}) %reduce-scatter.21.cloned.1.call-update) | async-done | bytes 1572880 | tf_op jit(solution)/shard_map/reduce_scatter | solution.py:210
  478.1 3.3 multiply_reduce_fusion.1
  485.0 23.1 %all_gather.60 = bf16[384,768]{0,1:T(8,128)(2,1)S(1)} all-gather(bf16[384,48]{0,1:T(8,128)(2,1)S(1)} %copy-done.23), channel_id=1, replica_groups=mesh['dp'=16,'tensor'=2] {'dp'}, dimensions={1}, use_global_device_ids=true | all-gather | bytes 626688 | tf_op jit(solution)/shard_map/all_gather | solution.py:190
  508.1 20.4 %all_gather.61 = bf16[768,384]{1,0:T(8,128)(2,1)} all-gather(bf16[48,384]{1,0:T(8,128)(2,1)S(1)} %copy-done.24), channel_id=1, replica_groups=mesh['dp'=16,'tensor'=2] {'dp'}, dimensions={0}, use_global_device_ids=true | all-gather | bytes 626688 | tf_op jit(solution)/shard_map/all_gather | solution.py:187
  528.6 22.0 %all_gather.62 = bf16[768,384]{1,0:T(8,128)(2,1)} all-gather(bf16[48,384]{1,0:T(8,128)(2,1)S(1)} %copy-done.25), channel_id=1, replica_groups=mesh['dp'=16,'tensor'=2] {'dp'}, dimensions={0}, use_global_device_ids=true | all-gather | bytes 626688 | tf_op jit(solution)/shard_map/all_gather | solution.py:188
  550.5 20.4 %all_gather.63 = bf16[768,384]{1,0:T(8,128)(2,1)} all-gather(bf16[48,384]{1,0:T(8,128)(2,1)S(1)} %copy-done.26), channel_id=1, replica_groups=mesh['dp'=16,'tensor'=2] {'dp'}, dimensions={0}, use_global_device_ids=true | all-gather | bytes 626688 | tf_op jit(solution)/shard_map/all_gather | solution.py:189
  571.0 3.1 convolution_convert_fusion
  575.1 57.7 %while.48 = (s32[]{:T(128)}, f32[1024,6,64]{0,2,1:T(8,128)S(1)}, f32[1024,6,64]{0,2,1:T(8,128)}, bf16[2,512,6,64]{1,3,2,0:T(8,128)(2,1)}, s32[2]{0:T(128)S(1)}, ...) while((s32[]{:T(128)}, f32[1024,6,64]{0,2,1:T(8,128)S(1)}, ...), condition=%wide.region_17.18_spmd.clone, body=%wide.region_15.17_spmd.clone.sunk | while | flops 2064906752 | bytes 144941456 | solution.py:93
  578.0 2.9 fusion.136
  580.9 4.6 bitcast_add_fusion.5
  585.5 5.4 multiply_reduce_fusion.6
  590.9 5.1 multiply_convert_fusion.3
  596.0 5.9 fusion.138
  606.1 2.9 fusion.136
  609.0 5.7 bitcast_add_fusion.5
  614.7 5.4 multiply_reduce_fusion.6
  620.1 5.1 multiply_convert_fusion.3
  625.2 5.9 fusion.138
  641.3 7.1 fusion.61
  648.5 7.2 fusion.60
  656.8 3.5 fusion.59
  673.5 39.8 %all-reduce = (f32[768]{0:T(1024)}, f32[768]{0:T(1024)}, f32[768]{0:T(1024)}, f32[768]{0:T(1024)}, f32[768]{0:T(1024)}, /*index=5*/f32[3072]{0:T(1024)}, f32[768]{0:T(1024)}, f32[768]{0:T(1024)}, f32[768]{0:T(1024)}) all-reduce(f32[768]{0:T(1024)S(1)} %dynamic_update_slice.32, ...), channel_id=1, replica_groups=mesh['dp'=16,'tensor'=2] {'dp','tensor'}, use_global_device_ids=true, to_apply=%region_21.22 | all-reduce | flops 9216 | bytes 73728 | tf_op jit(solution)/shard_map/psum | solution.py:274
  715.8 29.6 %reduce-scatter.29.cloned.1.call-done = f32[1536,48]{0,1:T(8,128)} async-done(((f32[1536,768]{0,1:T(8,128)}), f32[1536,48]{0,1:T(8,128)}) %reduce-scatter.29.cloned.1.call-update) | async-done | bytes 294928 | tf_op jit(solution)/shard_map/reduce_scatter | solution.py:267
  745.5 79.0 %reduce-scatter.27.cloned.1.call-done = f32[48,1536]{1,0:T(8,128)} async-done(((f32[768,1536]{1,0:T(8,128)}), f32[48,1536]{1,0:T(8,128)}) %reduce-scatter.27.cloned.1.call-update) | async-done | bytes 294928 | tf_op jit(solution)/shard_map/reduce_scatter | solution.py:266
  824.4 61.6 %reduce-scatter.25.cloned.1.call-done = f32[384,48]{0,1:T(8,128)} async-done(((f32[384,768]{0,1:T(8,128)}), f32[384,48]{0,1:T(8,128)}) %reduce-scatter.25.cloned.1.call-update) | async-done | bytes 73744 | tf_op jit(solution)/shard_map/reduce_scatter | solution.py:265
  886.1 61.4 %reduce-scatter.35.cloned.1.call-done = f32[48,384]{1,0:T(8,128)} async-done(((f32[768,384]{1,0:T(8,128)}), f32[48,384]{1,0:T(8,128)}) %reduce-scatter.35.cloned.1.call-update) | async-done | bytes 73744
  947.4 61.5 %reduce-scatter.31.cloned.1.call-done = f32[48,384]{1,0:T(8,128)} async-done(((f32[768,384]{1,0:T(8,128)}), f32[48,384]{1,0:T(8,128)}) %reduce-scatter.31.cloned.1.call-update) | async-done | bytes 73744
  1008.9 61.2 %reduce-scatter.33.cloned.1.call-done = f32[48,384]{1,0:T(8,128)} async-done(((f32[768,384]{1,0:T(8,128)}), f32[48,384]{1,0:T(8,128)}) %reduce-scatter.33.cloned.1.call-update) | async-done | bytes 73744
  (215 shorter events, 72.8 us)
Async XLA Ops:
  8.0 88.0 %all-gather.9.cloned.1.call-start = ((), (), s32[]{:S(2)}) async-start(), calls=%async_computation.10 | async-start | bytes 2359296 | tf_op jit(solution)/shard_map/all_gather | solution.py:146
  8.8 172.9 %reduce-scatter.17.cloned.1.call-start = ((), (), s32[]{:S(2)}) async-start(), calls=%async_computation.11 | async-start | bytes 4718592 | tf_op jit(solution)/shard_map/reduce_scatter | solution.py:167
  105.3 4.5 copy-start
  122.7 4.5 copy-start
  135.1 4.6 copy-start.6
  135.1 5.5 copy-start.4
  137.0 44.7 %copy-start.13 = (bf16[512,768]{1,0:T(8,128)(2,1)S(1)}, bf16[512,768]{1,0:T(8,128)(2,1)}, u32[]{:S(2)}) copy-start(bf16[512,768]{1,0:T(8,128)(2,1)} %param.23) | copy-start | bytes 2359300
  137.0 44.7 %copy-start.36 = (f32[768]{0:T(1024)S(1)}, f32[768]{0:T(1024)}, u32[]{:S(2)}) copy-start(f32[768]{0:T(1024)} %param.30) | copy-start | bytes 9220
  139.7 44.1 %copy-start.27 = (f32[768]{0:T(1024)S(1)}, f32[768]{0:T(1024)}, u32[]{:S(2)}) copy-start(f32[768]{0:T(1024)} %param.31) | copy-start | bytes 9220
  139.7 44.1 %copy-start.33 = (f32[768]{0:T(1024)S(1)}, f32[768]{0:T(1024)}, u32[]{:S(2)}) copy-start(f32[768]{0:T(1024)} %param.32) | copy-start | bytes 9220
  139.7 46.0 %all-gather.13.cloned.1.call-start = ((), (), s32[]{:S(2)}) async-start(), calls=%async_computation.13 | async-start | bytes 2506752 | tf_op jit(solution)/shard_map/all_gather | solution.py:143
  140.3 71.8 %all-gather.11.cloned.1.call-start = ((), (), s32[]{:S(2)}) async-start(), calls=%async_computation.12 | async-start | bytes 2359296 | tf_op jit(solution)/shard_map/all_gather | solution.py:170
  185.0 72.0 %all-gather.15.cloned.1.call-start = ((), (), s32[]{:S(2)}) async-start(), calls=%async_computation.14 | async-start | bytes 2506752 | tf_op jit(solution)/shard_map/all_gather | solution.py:144
  185.5 120.2 %reduce-scatter.19.cloned.1.call-start = ((), (), s32[]{:S(2)}) async-start(), calls=%async_computation.15 | async-start | bytes 4718592 | tf_op jit(solution)/shard_map/reduce_scatter | solution.py:174
  263.8 42.0 %copy-start.37 = (f32[768]{0:T(1024)S(1)}, f32[768]{0:T(1024)}, u32[]{:S(2)}) copy-start(f32[768]{0:T(1024)} %param.36) | copy-start | bytes 9220
  263.8 44.3 %copy-start.12 = (bf16[512,768]{1,0:T(8,128)(2,1)S(1)}, bf16[512,768]{1,0:T(8,128)(2,1)}, u32[]{:S(2)}) copy-start(bf16[512,768]{1,0:T(8,128)(2,1)} %param.41) | copy-start | bytes 2359300
  263.9 44.3 %copy-start.30 = (f32[768]{0:T(1024)S(1)}, f32[768]{0:T(1024)}, u32[]{:S(2)}) copy-start(f32[768]{0:T(1024)} %param.37) | copy-start | bytes 9220
  263.9 77.1 %all-gather.17.cloned.1.call-start = ((), (), s32[]{:S(2)}) async-start(), calls=%async_computation.16 | async-start | bytes 2359296 | tf_op jit(solution)/shard_map/all_gather | solution.py:194
  313.8 72.1 %all-gather.19.cloned.1.call-start = ((), (), s32[]{:S(2)}) async-start(), calls=%async_computation.17 | async-start | bytes 2506752 | tf_op jit(solution)/shard_map/all_gather | solution.py:192
  314.6 114.7 %all-gather.21.cloned.1.call-start = ((), (), s32[]{:S(2)}) async-start(), calls=%async_computation.18 | async-start | bytes 2506752 | tf_op jit(solution)/shard_map/all_gather | solution.py:191
  315.3 162.8 %reduce-scatter.21.cloned.1.call-start = ((), (), s32[]{:S(2)}) async-start(), calls=%async_computation.19 | async-start | bytes 4718592 | tf_op jit(solution)/shard_map/reduce_scatter | solution.py:210
  436.2 134.8 %all-gather.23.cloned.1.call-start = ((), (), s32[]{:S(2)}) async-start(), calls=%async_computation.20 | async-start | bytes 2359296 | tf_op jit(solution)/shard_map/all_gather | solution.py:216
  482.1 26.0 %copy-start.24 = (bf16[48,384]{1,0:T(8,128)(2,1)S(1)}, bf16[48,384]{1,0:T(8,128)(2,1)}, u32[]{:S(2)}) copy-start(bf16[48,384]{1,0:T(8,128)(2,1)} %param.24) | copy-start | bytes 110596
  482.1 46.5 %copy-start.25 = (bf16[48,384]{1,0:T(8,128)(2,1)S(1)}, bf16[48,384]{1,0:T(8,128)(2,1)}, u32[]{:S(2)}) copy-start(bf16[48,384]{1,0:T(8,128)(2,1)} %param.26) | copy-start | bytes 110596
  482.1 68.4 %copy-start.26 = (bf16[48,384]{1,0:T(8,128)(2,1)S(1)}, bf16[48,384]{1,0:T(8,128)(2,1)}, u32[]{:S(2)}) copy-start(bf16[48,384]{1,0:T(8,128)(2,1)} %param.27) | copy-start | bytes 110596
  484.9 228.4 %reduce-scatter.23.cloned.1.call-start = ((), (), s32[]{:S(2)}) async-start(), calls=%async_computation.21 | async-start | bytes 2359296 | tf_op jit(solution)/shard_map/reduce_scatter | solution.py:258
  575.2 5.7 copy-start.2
  578.0 2.9 copy-start.11
  596.0 5.9 copy-start.1
  596.0 5.9 copy-start.5
  603.3 5.7 copy-start.2
  606.1 2.9 copy-start.11
  625.1 5.9 copy-start.1
  625.2 5.9 copy-start.5
  632.8 5.1 copy-start.16
  632.9 4.0 copy-start.20
  641.2 104.2 %reduce-scatter.29.cloned.1.call-start = ((), (), s32[]{:S(2)}) async-start(), calls=%async_computation.24 | async-start | bytes 5013504 | tf_op jit(solution)/shard_map/reduce_scatter | solution.py:267
  648.4 176.0 %reduce-scatter.27.cloned.1.call-start = ((), (), s32[]{:S(2)}) async-start(), calls=%async_computation.23 | async-start | bytes 5013504 | tf_op jit(solution)/shard_map/reduce_scatter | solution.py:266
  655.7 230.4 %reduce-scatter.25.cloned.1.call-start = ((), (), s32[]{:S(2)}) async-start(), calls=%async_computation.22 | async-start | bytes 1253376 | tf_op jit(solution)/shard_map/reduce_scatter | solution.py:265
  660.4 287.1 %reduce-scatter.35.cloned.1.call-start = ((), (), s32[]{:S(2)}) async-start(), calls=%async_computation.27 | async-start | bytes 1253376
  664.1 4.1 copy-start.17
  664.1 344.8 %reduce-scatter.31.cloned.1.call-start = ((), (), s32[]{:S(2)}) async-start(), calls=%async_computation.25 | async-start | bytes 1253376
  667.8 4.9 copy-start.10
  667.8 402.3 %reduce-scatter.33.cloned.1.call-start = ((), (), s32[]{:S(2)}) async-start(), calls=%async_computation.26 | async-start | bytes 1253376
  670.3 3.1 copy-start.31
  670.4 3.1 copy-start.32
  670.4 43.0 %copy-start.8 = (f32[512,768]{1,0:T(8,128)S(1)}, f32[512,768]{1,0:T(8,128)}, u32[]{:S(2)}) copy-start(f32[512,768]{1,0:T(8,128)} %copy-done.7) | copy-start | bytes 4718596
  670.4 42.9 %copy-start.29 = (f32[512]{0:T(512)S(1)}, f32[512]{0:T(512)}, u32[]{:S(2)}) copy-start(f32[512]{0:T(512)} %copy-done.28) | copy-start | bytes 6148
  (15 other events, 25.7 us)
Sparse Core Ops, SparseCore 0:
  10.4 29.8 all-gather.8
  139.8 41.8 reduce-scatter.16
  264.0 41.7 reduce-scatter.18
  436.3 41.7 reduce-scatter.20
  485.0 27.1 all-gather.22
Sparse Core Ops, SparseCore 1:
  142.5 40.8 all-gather.12
  185.3 26.7 all-gather.10
  214.3 42.6 all-gather.14
  313.9 27.0 all-gather.16
  343.3 42.6 all-gather.18
  388.2 40.9 all-gather.20
  641.3 23.6 reduce-scatter.22
  669.3 76.1 reduce-scatter.28
  749.8 74.6 reduce-scatter.26
  828.7 57.3 reduce-scatter.24
  890.1 57.2 reduce-scatter.34
  951.6 57.2 reduce-scatter.30
  1013.0 57.1 reduce-scatter.32
where the time goes:
time: 1090 us; the launch traced here: 1080 us
  waiting for transfers between devices  635 us (58%)
  blocking collectives  212 us (19%)
  matrix products  147 us (13%)
  other arithmetic  42.9 us (4%)
  local copies, waits for them, and re-layouts  20.5 us (2%)
  between operations  16.7 us (2%)
    unnamed x21, waiting for transfers between devices  187 us
    reduce_scatter x1, waiting for transfers between devices, on_device(): lax.psum_scatter(inner_weight_grad, 'dp', scatter_dimension=0, tiled=True)  79 us
    reduce_scatter x1, waiting for transfers between devices, on_device(): lax.psum_scatter(output_weight_grad, 'dp', scatter_dimension=1, tiled=True)  61.6 us
    all_gather x1, waiting for transfers between devices, on_device(): lax.all_gather(held[5], 'dp', axis=1, tiled=True)  45 us
    reduce_scatter x1, waiting for transfers between devices, on_device(): lax.psum_scatter(partial_hidden, 'tensor', scatter_dimension=0, tiled=True)  41.9 us
    reduce_scatter x1, waiting for transfers between devices, on_device(): lax.psum_scatter(partial_ffn, 'tensor', scatter_dimension=0, tiled=True)  41.9 us
    reduce_scatter x1, waiting for transfers between devices, on_device(): lax.psum_scatter(partial_attn, 'tensor', scatter_dimension=0, tiled=True)  41.1 us
    psum x1, blocking collectives, on_device(): lax.psum((query_bias_full, value_bias_full, output_bias_grad, first_gain_...  39.8 us
  transfers between devices with their start and end apart: 18, of which 14 were waited for; matrix products, arithmetic and copies ran while one was open for 6% of the time, Pallas kernels for 0%

commit v1 on v0

--- a/solution.py
+++ b/solution.py
@@ -6,6 +6,28 @@
 HEAD_DIM = 64
 norm_epsilon = 1e-12
 masked_score = -1e30
+
+
+def in_order(pieces, dim):
+    pieces = jnp.moveaxis(pieces, 0, dim)
+    dims = pieces.shape
+    return pieces.reshape(*dims[:dim], dims[dim] * dims[dim + 1], *dims[dim + 2 :])
+
+
+def ring_gather(value, axis, dim):
+    size = lax.axis_size(axis)
+    pairs = [(i, (i + 1) % size) for i in range(size)]
+    back = [(b, a) for a, b in pairs]
+    lower, upper = ([], [])
+    for step in range(size - 1):
+        if step % 2 == 0:
+            lower.append(lax.ppermute(lower[-1] if lower else value, axis, pairs))
+        else:
+            upper.append(lax.ppermute(upper[-1] if upper else value, axis, back))
+    parts = jnp.stack([*lower[::-1], value, *upper])
+    shift = lax.axis_index(axis) - len(lower)
+    parts = parts[(jnp.arange(size) - shift) % size]
+    return in_order(parts, dim)
 
 
 def normalize(matrix, gain, shift):
@@ -189,7 +211,7 @@
         lax.all_gather(held[2], "dp", axis=0, tiled=True),
         lax.all_gather(held[3], "dp", axis=1, tiled=True),
         lax.all_gather(held[4], "dp", axis=0, tiled=True),
-        lax.all_gather(held[5], "dp", axis=1, tiled=True),
+        ring_gather(held[5], "dp", 1),
     )
     outer_grad_rows = lax.all_gather(d_outer, "tensor", axis=0, tiled=True)
     outer_weight_grad = jnp.einsum(

time: 1090 us -> 1070 us (0.982)
  waiting for transfers between devices: 635 us -> 565 us
  starting transfers between devices: 1.63 us -> 33.2 us
  local copies, waits for them, and re-layouts: 20.5 us -> 42.5 us
    all_gather x1 -> x0, waiting for transfers between devices: 45 us -> none  [on_device(): lax.all_gather(held[5], 'dp', axis=1, tiled=True)]
    ppermute x0 -> x15, starting transfers between devices: none -> 32 us  [the longest x7 31.9 us: ring_gather(): upper.append(lax.ppermute(upper[-1] if upper else value, axis, back))]
    all_gather x1, waiting for transfers between devices: 30.9 us -> 1.09 us  [on_device(): lax.all_gather(held[4], 'dp', axis=0, tiled=True)]
    ppermute x0 -> x15, waiting for transfers between devices: none -> 27.3 us  [the longest x8 27.2 us: ring_gather(): lower.append(lax.ppermute(lower[-1] if lower else value, axis, pairs))]
    all_gather x1, waiting for transfers between devices: 25.2 us -> 0.01 us  [on_device(): outer_grad_rows = lax.all_gather(d_outer, 'tensor', axis=0, tiled=True)]
    unnamed x71 -> x100, local copies, waits for them, and re-layouts: 8.76 us -> 27.8 us
    unnamed x21 -> x20, waiting for transfers between devices: 187 us -> 186 us
  transfers between devices with their start and end apart: 18 -> 32, of which waited for: 14 -> 21; matrix products, arithmetic and copies ran while one was open for 6% -> 8% of each run, Pallas kernels for 0% -> 0%
where the time goes in v1:
time: 1070 us; the launch traced here: 1060 us
  waiting for transfers between devices  565 us (53%)
  blocking collectives  211 us (20%)
  matrix products  144 us (13%)
  other arithmetic  42.9 us (4%)
  local copies, waits for them, and re-layouts  42.5 us (4%)
  starting transfers between devices  33.2 us (3%)
  between operations  16.7 us (2%)
    unnamed x20, waiting for transfers between devices  186 us
    reduce_scatter x1, waiting for transfers between devices, on_device(): lax.psum_scatter(inner_weight_grad, 'dp', scatter_dimension=0, tiled=True)  79 us
    reduce_scatter x1, waiting for transfers between devices, on_device(): lax.psum_scatter(output_weight_grad, 'dp', scatter_dimension=1, tiled=True)  61.9 us
    reduce_scatter x1, waiting for transfers between devices, on_device(): lax.psum_scatter(partial_hidden, 'tensor', scatter_dimension=0, tiled=True)  41.9 us
    reduce_scatter x1, waiting for transfers between devices, on_device(): lax.psum_scatter(partial_ffn, 'tensor', scatter_dimension=0, tiled=True)  41.9 us
    reduce_scatter x1, waiting for transfers between devices, on_device(): lax.psum_scatter(partial_attn, 'tensor', scatter_dimension=0, tiled=True)  41.2 us
    psum x1, blocking collectives, on_device(): lax.psum((query_bias_full, value_bias_full, output_bias_grad, first_gain_...  39.2 us
    reduce_scatter x1, waiting for transfers between devices, on_device(): lax.psum_scatter(outer_weight_grad, 'dp', scatter_dimension=1, tiled=True)  32.7 us
  transfers between devices with their start and end apart: 32, of which 21 were waited for; matrix products, arithmetic and copies ran while one was open for 8% of the time, Pallas kernels for 0%

profile of v1, /device:TPU:0, one launch (start us, length us, event | category | flops | bytes accessed | tf_op | source)
XLA Modules:
  0.0 1057.5 jit_solution(14836828708076920084)
XLA Ops:
  10.4 25.1 %all_gather.46 = bf16[768,384]{1,0:T(8,128)(2,1)S(1)} all-gather(bf16[48,384]{1,0:T(8,128)(2,1)} %param.24), channel_id=1, replica_groups=mesh['dp'=16,'tensor'=2] {'dp'}, dimensions={0}, use_global_device_ids=true | all-gather | bytes 626688 | tf_op jit(solution)/shard_map/all_gather | solution.py:161
  35.4 19.3 %all_gather.47 = bf16[768,384]{1,0:T(8,128)(2,1)S(1)} all-gather(bf16[48,384]{1,0:T(8,128)(2,1)} %param.26), channel_id=1, replica_groups=mesh['dp'=16,'tensor'=2] {'dp'}, dimensions={0}, use_global_device_ids=true | all-gather | bytes 626688 | tf_op jit(solution)/shard_map/all_gather | solution.py:162
  54.7 20.7 %all_gather.48 = bf16[768,384]{1,0:T(8,128)(2,1)S(1)} all-gather(bf16[48,384]{1,0:T(8,128)(2,1)} %param.27), channel_id=1, replica_groups=mesh['dp'=16,'tensor'=2] {'dp'}, dimensions={0}, use_global_device_ids=true | all-gather | bytes 626688 | tf_op jit(solution)/shard_map/all_gather | solution.py:163
  75.4 20.4 %all_gather.49 = bf16[384,768]{0,1:T(8,128)(2,1)} all-gather(bf16[384,48]{0,1:T(8,128)(2,1)S(1)} %copy-done.25), channel_id=1, replica_groups=mesh['dp'=16,'tensor'=2] {'dp'}, dimensions={1}, use_global_device_ids=true | all-gather | bytes 626688 | tf_op jit(solution)/shard_map/all_gather | solution.py:164
  100.0 34.8 %while.47 = (s32[]{:T(128)}, bf16[2,512,6,64]{1,3,2,0:T(8,128)(2,1)S(1)}, f32[2,6,512]{2,1,0:T(8,128)S(1)}, s32[2]{0:T(128)S(1)}, s32[1024]{0:T(1024)S(1)}, /*in...) while((s32[]{:T(128)}, ...), condition=%wide.region_3.4_spmd, body=%wide.region_0.3_spmd.sunk | while | flops 842201600 | bytes 92672240 | solution.py:76
  105.1 3.6 exponential_reduce_fusion.2
  109.6 7.8 fusion.128
  127.0 7.8 fusion.128
  140.2 41.2 %reduce-scatter.17.cloned.1.call-done = f32[512,768]{1,0:T(8,128)} async-done(((f32[1024,768]{1,0:T(8,128)}), f32[512,768]{1,0:T(8,128)}) %reduce-scatter.17.cloned.1.call-update) | async-done | bytes 1572880 | tf_op jit(solution)/shard_map/reduce_scatter | solution.py:189
  185.4 26.4 %all-gather.10.cloned.1.call-done = bf16[1024,768]{1,0:T(8,128)(2,1)} async-done(((bf16[512,768]{1,0:T(8,128)(2,1)}), bf16[1024,768]{1,0:T(8,128)(2,1)}) %all-gather.10.cloned.1.call-update) | async-done | bytes 1572880 | tf_op jit(solution)/shard_map/all_gather | solution.py:192
  211.9 19.9 %multiply_convert_fusion.1 = (bf16[1024,1536]{1,0:T(8,128)(2,1)}, f32[1024,1536]{1,0:T(8,128)}, f32[1024,1536]{1,0:T(8,128)}) fusion(f32[1536]{0:T(1024)S(1)} %dynamic_slice.65, bf16[1024,768]{1,0:T(8,128)(2,1)} %all-gather.10.cloned.1.call-done, bf16[768,1536]{1,0:T(8,128)(2,1)} %all-gather.12.cloned.1.call-done), kind=kOutput, calls=%fused_computation.56 | convolution fusion | flops 2519728128 | bytes 19666944 | tf_op jit(solution)/shard_map/dot_general | solution.py:193
  231.8 24.9 %all-gather.14.cloned.1.call-done = bf16[1536,768]{0,1:T(8,128)(2,1)} async-done(((bf16[1536,48]{0,1:T(8,128)(2,1)}), bf16[1536,768]{0,1:T(8,128)(2,1)}) %all-gather.14.cloned.1.call-update) | async-done | bytes 2359312 | tf_op jit(solution)/shard_map/all_gather | solution.py:166
  256.7 6.9 fusion.57
  263.7 41.9 %reduce-scatter.19.cloned.1.call-done = f32[512,768]{1,0:T(8,128)} async-done(((f32[1024,768]{1,0:T(8,128)}), f32[512,768]{1,0:T(8,128)}) %reduce-scatter.19.cloned.1.call-update) | async-done | bytes 1572880 | tf_op jit(solution)/shard_map/reduce_scatter | solution.py:196
  313.7 7.3 collective-permute-done
  320.9 4.4 collective-permute-start.8
  328.2 4.4 collective-permute-start.9
  335.6 4.4 collective-permute-start.10
  342.9 4.4 collective-permute-start.11
  350.3 4.5 collective-permute-start.12
  357.8 4.7 collective-permute-start.13
  365.6 4.9 collective-permute-start.14
  391.0 3.8 gather_fusion
  394.8 12.5 %convert_reduce_fusion = (f32[1536]{0:T(1024)}, bf16[1024,1536]{1,0:T(8,128)(2,1)}) fusion(f32[1024,1536]{1,0:T(8,128)} %get-tuple-element.366, f32[1024,1536]{1,0:T(8,128)} %get-tuple-element.378, f32[1536]{0:T(1024)S(1)} %dynamic_slice.65, bf16[1024,768]{1,0:T(8,128)(2,1)} %all-gather.16.cloned.1.call-done, bf16[1536,768]{0,1:T(8,128)(2,1)} %bitcast.162), kind=kOutput, calls=%fused_computation.54 | convolution fusion | flops 2442656256 | bytes 19673088 | tf_op jit(solution)/shard_map/gd,fd->gf/dot_general | solution.py:220
  408.4 6.9 fusion.58
  415.4 41.9 %reduce-scatter.21.cloned.1.call-done = f32[512,768]{1,0:T(8,128)} async-done(((f32[1024,768]{1,0:T(8,128)}), f32[512,768]{1,0:T(8,128)}) %reduce-scatter.21.cloned.1.call-update) | async-done | bytes 1572880 | tf_op jit(solution)/shard_map/reduce_scatter | solution.py:232
  464.2 23.1 %all_gather.56 = bf16[384,768]{0,1:T(8,128)(2,1)S(1)} all-gather(bf16[384,48]{0,1:T(8,128)(2,1)S(1)} %copy-done.26), channel_id=1, replica_groups=mesh['dp'=16,'tensor'=2] {'dp'}, dimensions={1}, use_global_device_ids=true | all-gather | bytes 626688 | tf_op jit(solution)/shard_map/all_gather | solution.py:212
  487.3 20.4 %all_gather.57 = bf16[768,384]{1,0:T(8,128)(2,1)} all-gather(bf16[48,384]{1,0:T(8,128)(2,1)S(1)} %copy-done.27), channel_id=1, replica_groups=mesh['dp'=16,'tensor'=2] {'dp'}, dimensions={0}, use_global_device_ids=true | all-gather | bytes 626688 | tf_op jit(solution)/shard_map/all_gather | solution.py:209
  507.7 22.0 %all_gather.58 = bf16[768,384]{1,0:T(8,128)(2,1)} all-gather(bf16[48,384]{1,0:T(8,128)(2,1)S(1)} %copy-done.28), channel_id=1, replica_groups=mesh['dp'=16,'tensor'=2] {'dp'}, dimensions={0}, use_global_device_ids=true | all-gather | bytes 626688 | tf_op jit(solution)/shard_map/all_gather | solution.py:210
  529.7 20.4 %all_gather.59 = bf16[768,384]{1,0:T(8,128)(2,1)} all-gather(bf16[48,384]{1,0:T(8,128)(2,1)S(1)} %copy-done.29), channel_id=1, replica_groups=mesh['dp'=16,'tensor'=2] {'dp'}, dimensions={0}, use_global_device_ids=true | all-gather | bytes 626688 | tf_op jit(solution)/shard_map/all_gather | solution.py:211
  554.2 57.7 %while.48 = (s32[]{:T(128)}, f32[1024,6,64]{0,2,1:T(8,128)S(1)}, f32[1024,6,64]{0,2,1:T(8,128)}, bf16[2,512,6,64]{1,3,2,0:T(8,128)(2,1)}, s32[2]{0:T(128)S(1)}, ...) while((s32[]{:T(128)}, f32[1024,6,64]{0,2,1:T(8,128)S(1)}, ...), condition=%wide.region_17.18_spmd.clone, body=%wide.region_15.17_spmd.clone.sunk | while | flops 2064906752 | bytes 144941456 | solution.py:115
  560.1 4.6 bitcast_add_fusion.5
  564.6 5.4 multiply_reduce_fusion.6
  570.0 5.1 multiply_convert_fusion.3
  575.2 5.9 fusion.140
  588.2 5.7 bitcast_add_fusion.5
  593.9 5.4 multiply_reduce_fusion.6
  599.2 5.1 multiply_convert_fusion.3
  604.4 5.9 fusion.140
  620.3 7.2 fusion.63
  627.5 7.2 fusion.62
  650.0 39.2 %all-reduce = (f32[768]{0:T(1024)}, f32[768]{0:T(1024)}, f32[768]{0:T(1024)}, f32[768]{0:T(1024)}, f32[768]{0:T(1024)}, /*index=5*/f32[3072]{0:T(1024)}, f32[768]{0:T(1024)}, f32[768]{0:T(1024)}, f32[768]{0:T(1024)}) all-reduce(f32[768]{0:T(1024)S(1)} %dynamic_update_slice.32, ...), channel_id=1, replica_groups=mesh['dp'=16,'tensor'=2] {'dp','tensor'}, use_global_device_ids=true, to_apply=%region_21.22 | all-reduce | flops 9216 | bytes 73728 | tf_op jit(solution)/shard_map/psum | solution.py:296
  691.7 32.7 %reduce-scatter.29.cloned.1.call-done = f32[1536,48]{0,1:T(8,128)} async-done(((f32[1536,768]{0,1:T(8,128)}), f32[1536,48]{0,1:T(8,128)}) %reduce-scatter.29.cloned.1.call-update) | async-done | bytes 294928 | tf_op jit(solution)/shard_map/reduce_scatter | solution.py:289
  724.4 79.0 %reduce-scatter.27.cloned.1.call-done = f32[48,1536]{1,0:T(8,128)} async-done(((f32[768,1536]{1,0:T(8,128)}), f32[48,1536]{1,0:T(8,128)}) %reduce-scatter.27.cloned.1.call-update) | async-done | bytes 294928 | tf_op jit(solution)/shard_map/reduce_scatter | solution.py:288
  803.4 61.9 %reduce-scatter.25.cloned.1.call-done = f32[384,48]{0,1:T(8,128)} async-done(((f32[384,768]{0,1:T(8,128)}), f32[384,48]{0,1:T(8,128)}) %reduce-scatter.25.cloned.1.call-update) | async-done | bytes 73744 | tf_op jit(solution)/shard_map/reduce_scatter | solution.py:287
  865.3 61.4 %reduce-scatter.35.cloned.1.call-done = f32[48,384]{1,0:T(8,128)} async-done(((f32[768,384]{1,0:T(8,128)}), f32[48,384]{1,0:T(8,128)}) %reduce-scatter.35.cloned.1.call-update) | async-done | bytes 73744
  926.7 61.6 %reduce-scatter.31.cloned.1.call-done = f32[48,384]{1,0:T(8,128)} async-done(((f32[768,384]{1,0:T(8,128)}), f32[48,384]{1,0:T(8,128)}) %reduce-scatter.31.cloned.1.call-update) | async-done | bytes 73744
  988.3 61.4 %reduce-scatter.33.cloned.1.call-done = f32[48,384]{1,0:T(8,128)} async-done(((f32[768,384]{1,0:T(8,128)}), f32[48,384]{1,0:T(8,128)}) %reduce-scatter.33.cloned.1.call-update) | async-done | bytes 73744
  (275 shorter events, 126.8 us)
Async XLA Ops:
  8.0 67.4 %copy-start.25 = (bf16[384,48]{0,1:T(8,128)(2,1)S(1)}, bf16[384,48]{0,1:T(8,128)(2,1)}, u32[]{:S(2)}) copy-start(bf16[384,48]{0,1:T(8,128)(2,1)} %param.29) | copy-start | bytes 110596
  8.0 87.8 %all-gather.8.cloned.1.call-start = ((), (), s32[]{:S(2)}) async-start(), calls=%async_computation.10 | async-start | bytes 2359296 | tf_op jit(solution)/shard_map/all_gather | solution.py:168
  8.8 172.7 %reduce-scatter.17.cloned.1.call-start = ((), (), s32[]{:S(2)}) async-start(), calls=%async_computation.11 | async-start | bytes 4718592 | tf_op jit(solution)/shard_map/reduce_scatter | solution.py:189
  139.3 42.1 %copy-start.14 = (bf16[512,768]{1,0:T(8,128)(2,1)S(1)}, bf16[512,768]{1,0:T(8,128)(2,1)}, u32[]{:S(2)}) copy-start(bf16[512,768]{1,0:T(8,128)(2,1)} %param.23) | copy-start | bytes 2359300
  139.3 42.1 %copy-start.41 = (f32[768]{0:T(1024)S(1)}, f32[768]{0:T(1024)}, u32[]{:S(2)}) copy-start(f32[768]{0:T(1024)} %param.30) | copy-start | bytes 9220
  139.4 46.1 %all-gather.12.cloned.1.call-start = ((), (), s32[]{:S(2)}) async-start(), calls=%async_computation.13 | async-start | bytes 2506752 | tf_op jit(solution)/shard_map/all_gather | solution.py:165
  140.0 43.5 %copy-start.32 = (f32[768]{0:T(1024)S(1)}, f32[768]{0:T(1024)}, u32[]{:S(2)}) copy-start(f32[768]{0:T(1024)} %param.31) | copy-start | bytes 9220
  140.0 43.5 %copy-start.38 = (f32[768]{0:T(1024)S(1)}, f32[768]{0:T(1024)}, u32[]{:S(2)}) copy-start(f32[768]{0:T(1024)} %param.32) | copy-start | bytes 9220
  140.0 71.9 %all-gather.10.cloned.1.call-start = ((), (), s32[]{:S(2)}) async-start(), calls=%async_computation.12 | async-start | bytes 2359296 | tf_op jit(solution)/shard_map/all_gather | solution.py:192
  184.7 72.0 %all-gather.14.cloned.1.call-start = ((), (), s32[]{:S(2)}) async-start(), calls=%async_computation.14 | async-start | bytes 2506752 | tf_op jit(solution)/shard_map/all_gather | solution.py:166
  185.3 120.3 %reduce-scatter.19.cloned.1.call-start = ((), (), s32[]{:S(2)}) async-start(), calls=%async_computation.15 | async-start | bytes 4718592 | tf_op jit(solution)/shard_map/reduce_scatter | solution.py:196
  263.6 42.0 %copy-start.42 = (f32[768]{0:T(1024)S(1)}, f32[768]{0:T(1024)}, u32[]{:S(2)}) copy-start(f32[768]{0:T(1024)} %param.36) | copy-start | bytes 9220
  263.6 44.3 %copy-start.13 = (bf16[512,768]{1,0:T(8,128)(2,1)S(1)}, bf16[512,768]{1,0:T(8,128)(2,1)}, u32[]{:S(2)}) copy-start(bf16[512,768]{1,0:T(8,128)(2,1)} %param.41) | copy-start | bytes 2359300
  263.6 44.3 %copy-start.35 = (f32[768]{0:T(1024)S(1)}, f32[768]{0:T(1024)}, u32[]{:S(2)}) copy-start(f32[768]{0:T(1024)} %param.37) | copy-start | bytes 9220
  263.6 131.2 %all-gather.16.cloned.1.call-start = ((), (), s32[]{:S(2)}) async-start(), calls=%async_computation.16 | async-start | bytes 2359296 | tf_op jit(solution)/shard_map/all_gather | solution.py:216
  313.5 94.9 %all-gather.18.cloned.1.call-start = ((), (), s32[]{:S(2)}) async-start(), calls=%async_computation.17 | async-start | bytes 2506752 | tf_op jit(solution)/shard_map/all_gather | solution.py:213
  313.6 7.3 collective-permute-start
  320.9 7.3 collective-permute-start.1
  320.9 7.3 collective-permute-start.8
  328.2 7.4 collective-permute-start.2
  328.2 7.4 collective-permute-start.9
  335.6 7.4 collective-permute-start.3
  335.6 7.4 collective-permute-start.10
  342.9 7.4 copy-start.30
  342.9 7.4 collective-permute-start.4
  342.9 7.4 collective-permute-start.11
  350.3 7.5 collective-permute-start.5
  350.3 7.5 collective-permute-start.12
  357.8 7.7 collective-permute-start.6
  357.8 7.7 collective-permute-start.13
  365.5 7.6 collective-permute-start.7
  365.5 91.8 %reduce-scatter.21.cloned.1.call-start = ((), (), s32[]{:S(2)}) async-start(), calls=%async_computation.18 | async-start | bytes 4718592 | tf_op jit(solution)/shard_map/reduce_scatter | solution.py:232
  365.6 24.8 %collective-permute-start.14 = (bf16[1536,48]{0,1:T(8,128)(2,1)}, bf16[1536,48]{0,1:T(8,128)(2,1)S(1)}, u32[]{:S(2)}, u32[]{:S(2)}) collective-permute-start(bf16[1536,48]{0,1:T(8,128)(2,1)} %collective-permute-done.13), channel_id=1, source_target_pairs={{2,0},{4,2},{6,4},{8,6},{10,8},{12,10},{14,12},{16,14},{18,16},{20... | collective-permute-start | bytes 442376 | tf_op jit(solution)/shard_map/ppermute | solution.py:26
  415.3 134.8 %all-gather.20.cloned.1.call-start = ((), (), s32[]{:S(2)}) async-start(), calls=%async_computation.19 | async-start | bytes 2359296 | tf_op jit(solution)/shard_map/all_gather | solution.py:238
  461.2 26.1 %copy-start.27 = (bf16[48,384]{1,0:T(8,128)(2,1)S(1)}, bf16[48,384]{1,0:T(8,128)(2,1)}, u32[]{:S(2)}) copy-start(bf16[48,384]{1,0:T(8,128)(2,1)} %param.24) | copy-start | bytes 110596
  461.2 46.5 %copy-start.28 = (bf16[48,384]{1,0:T(8,128)(2,1)S(1)}, bf16[48,384]{1,0:T(8,128)(2,1)}, u32[]{:S(2)}) copy-start(bf16[48,384]{1,0:T(8,128)(2,1)} %param.26) | copy-start | bytes 110596
  462.4 67.3 %copy-start.29 = (bf16[48,384]{1,0:T(8,128)(2,1)S(1)}, bf16[48,384]{1,0:T(8,128)(2,1)}, u32[]{:S(2)}) copy-start(bf16[48,384]{1,0:T(8,128)(2,1)} %param.27) | copy-start | bytes 110596
  464.1 225.1 %reduce-scatter.23.cloned.1.call-start = ((), (), s32[]{:S(2)}) async-start(), calls=%async_computation.20 | async-start | bytes 2359296 | tf_op jit(solution)/shard_map/reduce_scatter | solution.py:280
  604.4 5.9 copy-start.1
  604.4 5.9 copy-start.5
  620.2 104.2 %reduce-scatter.29.cloned.1.call-start = ((), (), s32[]{:S(2)}) async-start(), calls=%async_computation.23 | async-start | bytes 5013504 | tf_op jit(solution)/shard_map/reduce_scatter | solution.py:289
  627.4 176.0 %reduce-scatter.27.cloned.1.call-start = ((), (), s32[]{:S(2)}) async-start(), calls=%async_computation.22 | async-start | bytes 5013504 | tf_op jit(solution)/shard_map/reduce_scatter | solution.py:288
  634.7 230.6 %reduce-scatter.25.cloned.1.call-start = ((), (), s32[]{:S(2)}) async-start(), calls=%async_computation.21 | async-start | bytes 1253376 | tf_op jit(solution)/shard_map/reduce_scatter | solution.py:287
  639.3 287.4 %reduce-scatter.35.cloned.1.call-start = ((), (), s32[]{:S(2)}) async-start(), calls=%async_computation.26 | async-start | bytes 1253376
  643.0 345.3 %reduce-scatter.31.cloned.1.call-start = ((), (), s32[]{:S(2)}) async-start(), calls=%async_computation.24 | async-start | bytes 1253376
  645.4 404.3 %reduce-scatter.33.cloned.1.call-start = ((), (), s32[]{:S(2)}) async-start(), calls=%async_computation.25 | async-start | bytes 1253376
  646.9 42.3 %copy-start.8 = (f32[512,768]{1,0:T(8,128)S(1)}, f32[512,768]{1,0:T(8,128)}, u32[]{:S(2)}) copy-start(f32[512,768]{1,0:T(8,128)} %copy-done.7) | copy-start | bytes 4718596
  646.9 42.3 %copy-start.34 = (f32[512]{0:T(512)S(1)}, f32[512]{0:T(512)}, u32[]{:S(2)}) copy-start(f32[512]{0:T(512)} %copy-done.33) | copy-start | bytes 6148
  (36 other events, 100.6 us)
Sparse Core Ops, SparseCore 0:
  10.4 29.8 all-gather.7
  139.5 41.8 reduce-scatter.16
  263.7 41.7 reduce-scatter.18
  415.5 41.7 reduce-scatter.20
Sparse Core Ops, SparseCore 1:
  142.1 40.8 all-gather.11
  185.0 26.8 all-gather.9
  214.0 42.6 all-gather.13
  313.6 27.0 all-gather.15
  365.6 42.8 all-gather.17
  464.1 27.0 all-gather.19
  620.3 23.6 reduce-scatter.22
  648.2 76.1 reduce-scatter.28
  728.7 74.7 reduce-scatter.26
  807.6 57.6 reduce-scatter.24
  869.4 57.3 reduce-scatter.34
  930.9 57.3 reduce-scatter.30
  992.4 57.3 reduce-scatter.32
